TPU v7x, 256 devices: a whole 4x4x8 slice. The times are simulated.
256 devices in a mesh: path: 32 (over x, z), mp: 2 (over core), period: 4 (over y).
Axes of the slice: x: 4, y: 4, z: 8, core: 2. Of those that a mesh axis runs over, the one named last changes fastest.
Arguments:
- tiles: bfloat16 [4096, 256, 256], P(('path', 'mp')), may hold values from -0.375 to 0.375
- tile_rows: int32 [4096], P(('path', 'mp')), may hold values from 0 to 7
- tile_cols: int32 [4096], P(('path', 'mp')), may hold values from 0 to 1023, as said below
- tile_counts: int32 [64], P(('path', 'mp')), may hold values from 8 to 64, as said below
- data: float32 [262144], P(('period', 'path')), parts along dimension 0, may hold values from -6 to 6
Outputs:
- solution: float32 [2097152], P(('period', 'path', 'mp')), parts along dimension 0
- left_vector: float32 [262144], P(('period', 'path')), parts along dimension 0
There are 4 independent parts, one for each index of `period`. A program takes and returns all parts, laid end to end along the dimension named above; an argument that names none is the same for every part. Nothing has to cross between parts.
Inputs may be any that keep to these rules, and one draw needn't show every extreme that they name: `tile_counts`: slots from the strip's count on are unused; some strips are full. `tile_cols`: among all 64 slots of one strip, at most 8 name cell tiles t with the same t // 32, and in every strip some value of t // 32 is named by exactly 8 slots.
All inputs are finite; a program needn't handle non-finite values.
Results may differ from a plain program's by a relative error of at most 0.0066.
Values may be sent and summed in bfloat16 or wider, within the bound.
No kernel may reach another device: no remote copies, remote signals or barrier semaphores. Data moves between devices by JAX's collectives and lax.ppermute only.
A program may use at most 64 MiB of HBM per device.

v0:
```python
import jax
import jax.numpy as jnp
from jax import lax
from jax.sharding import PartitionSpec as P

CT_DEV = 32
ITERS = 2


def on_device(tiles, tile_rows, tile_cols, tile_counts, data):
    tile = tiles.shape[1]
    slots = tiles.shape[0]
    row_tiles = data.shape[0] // tile
    npath = lax.axis_size("path")
    half_tiles = CT_DEV * npath
    limit = max(2, max(slots // 8, (slots + npath - 1) // npath))
    live = lax.iota(jnp.int32, slots) < tile_counts[0]
    row_onehot = (
        (tile_rows[None, :] == lax.iota(jnp.int32, row_tiles)[:, None]) & live[None, :]
    ).astype(jnp.float32)
    col_onehot = (
        (tile_cols[None, :] == lax.iota(jnp.int32, half_tiles)[:, None]) & live[None, :]
    ).astype(jnp.float32)
    owner = tile_cols // CT_DEV
    inside = tile_cols % CT_DEV
    same_owner = (owner[:, None] == owner[None, :]).astype(jnp.int32)
    earlier = (lax.iota(jnp.int32, slots)[None, :] < lax.iota(jnp.int32, slots)[:, None]).astype(
        jnp.int32
    )
    rank = jnp.sum(same_owner * earlier, axis=1)
    target = owner * limit + rank
    place = lax.iota(jnp.int32, npath * limit)[:, None] == target[None, :]
    place_live = (place & live[None, :]).astype(jnp.float32)
    slot_inside = (
        jnp.sum(jnp.where(place, inside[None, :], 0), axis=1)
        - 1
        + jnp.sum(place.astype(jnp.int32), axis=1)
    )
    send_index = jnp.where(jnp.sum(place_live, axis=1) > 0, slot_inside, -1).reshape(npath, limit)

    def forward_prods(picked):
        prods = jnp.einsum("sij,sj->si", tiles, picked, preferred_element_type=jnp.float32)
        local = jnp.dot(row_onehot, prods, precision=lax.Precision.HIGHEST).reshape(-1)
        return lax.psum(local, "mp")

    def backward_prods(left_b):
        picked = left_b.reshape(row_tiles, tile)[tile_rows]
        return jnp.einsum("sij,si->sj", tiles, picked, preferred_element_type=jnp.float32)

    def row_norm(left):
        return jnp.sqrt(lax.psum(jnp.sum(left * left), "path") + 1e-12)

    def col_norm(own):
        return jnp.sqrt(lax.psum(jnp.sum(own * own), ("path", "mp")) + 1e-12)

    def right_step(left, state, beta, asked):
        prods = backward_prods(left.astype(jnp.bfloat16))
        partial_cols = jnp.dot(col_onehot, prods, precision=lax.Precision.HIGHEST).reshape(-1)
        own = lax.psum_scatter(partial_cols, "path", scatter_dimension=0, tiled=True)
        if state is not None:
            own = own - beta * state
        alpha = col_norm(own)
        own = own / alpha
        return (own, own, alpha, asked)

    beta = row_norm(data)
    left = data / beta
    phibar = beta
    asked = send_index
    state, right, alpha, asked = right_step(left, None, beta, asked)
    search = right
    rhobar = alpha
    solution = jnp.zeros_like(right)
    for step in range(ITERS):
        half_b = lax.all_gather(state.astype(jnp.bfloat16), "path", axis=0, tiled=True)
        forward_picked = half_b.reshape(half_tiles, tile)[tile_cols]
        left = forward_prods(forward_picked) - alpha * left
        beta = row_norm(left)
        left = left / beta
        state, right, alpha, asked = right_step(left, state, beta, asked)
        rho = jnp.sqrt(rhobar * rhobar + beta * beta)
        cosine = rhobar / rho
        sine = beta / rho
        theta = sine * alpha
        rhobar = -cosine * alpha
        phi = cosine * phibar
        phibar = sine * phibar
        solution = solution + phi / rho * search
        search = right - theta / rho * search
    total_rows = row_tiles * tile * npath
    return (solution, left * jnp.sqrt(jnp.float32(total_rows)))


def solution(mesh):
    placed = (
        P(("path", "mp"), None, None),
        P(("path", "mp")),
        P(("path", "mp")),
        P(("path", "mp")),
        P(("period", "path")),
    )
    return jax.shard_map(
        on_device,
        mesh=mesh,
        in_specs=placed,
        out_specs=(P(("period", "path", "mp")), P(("period", "path"))),
        check_vma=False,
    )
```

profile of v0, /device:TPU:8, one launch (start us, length us, event | category | flops | bytes accessed | tf_op | source)
XLA Modules:
  0.0 916.7 jit_solution(12098558276543920752)
XLA Ops:
  7.2 1.3 multiply_reduce_fusion.4
  8.5 78.3 %psum.49 = f32[]{:T(128)} all-reduce(f32[]{:T(128)} %multiply_reduce_fusion.4), channel_id=1, replica_groups=mesh['path'=32,'mp'=2,'period'=4] {'path'}, use_global_device_ids=true, to_apply=%region_1.0 | all-reduce | flops 1 | bytes 8 | tf_op jit(solution)/shard_map/psum | solution.py:51
  87.5 0.7 fusion.27
  88.2 0.7 compare_select_fusion.1
  89.6 0.7 gather_fusion
  90.3 4.6 fusion.21
  95.4 1.6 copy.15
  98.3 143.1 %all-reduce.5.cloned.1.call-done = f32[262144]{0:T(1024)} async-done(((f32[262144]{0:T(1024)}), f32[262144]{0:T(1024)}) %all-reduce.5.cloned.1.call-update) | async-done | bytes 1048592
  241.5 1.4 multiply_reduce_fusion.1
  242.8 124.7 %psum.50 = f32[]{:T(128)} all-reduce(f32[]{:T(128)} %multiply_reduce_fusion.1), channel_id=1, replica_groups=mesh['path'=32,'mp'=2,'period'=4] {'path','mp'}, use_global_device_ids=true, to_apply=%region_4.0 | all-reduce | flops 1 | bytes 8 | tf_op jit(solution)/shard_map/psum | solution.py:54
  368.2 0.8 fusion.33
  369.0 46.3 %all_gather.6 = bf16[262144]{0:T(1024)(128)(2,1)S(1)} all-gather(bf16[8192]{0:T(1024)(128)(2,1)S(1)} %fusion.33), channel_id=1, replica_groups=mesh['path'=32,'mp'=2,'period'=4] {'path'}, dimensions={0}, use_global_device_ids=true | all-gather | bytes 540672 | tf_op jit(solution)/shard_map/all_gather | solution.py:75
  415.5 0.7 gather_fusion.1
  416.2 5.6 fusion.18
  422.0 2.5 psum.51
  424.5 0.6 multiply_reduce_fusion.3
  425.1 72.9 %psum.52 = f32[]{:T(128)} all-reduce(f32[]{:T(128)} %get-tuple-element.2), channel_id=1, replica_groups=mesh['path'=32,'mp'=2,'period'=4] {'path'}, use_global_device_ids=true, to_apply=%region_7.0 | all-reduce | flops 1 | bytes 8 | tf_op jit(solution)/shard_map/psum | solution.py:51
  498.7 0.7 gather_fusion.2
  499.4 4.6 fusion.15
  504.6 1.5 copy.17
  506.3 144.1 %all-reduce.7.cloned.1.call-done = f32[262144]{0:T(1024)} async-done(((f32[262144]{0:T(1024)}), f32[262144]{0:T(1024)}) %all-reduce.7.cloned.1.call-update) | async-done | bytes 1048592
  650.3 1.4 multiply_reduce_fusion
  651.8 124.7 %psum.53 = f32[]{:T(128)} all-reduce(f32[]{:T(128)} %multiply_reduce_fusion), channel_id=1, replica_groups=mesh['path'=32,'mp'=2,'period'=4] {'path','mp'}, use_global_device_ids=true, to_apply=%region_10.0 | all-reduce | flops 1 | bytes 8 | tf_op jit(solution)/shard_map/psum | solution.py:54
  777.2 0.8 fusion.23
  778.0 46.3 %all_gather.7 = bf16[262144]{0:T(1024)(128)(2,1)S(1)} all-gather(bf16[8192]{0:T(1024)(128)(2,1)S(1)} %fusion.23), channel_id=1, replica_groups=mesh['path'=32,'mp'=2,'period'=4] {'path'}, dimensions={0}, use_global_device_ids=true | all-gather | bytes 540672 | tf_op jit(solution)/shard_map/all_gather | solution.py:75
  824.5 0.7 gather_fusion.3
  825.2 5.6 fusion.12
  831.0 2.5 psum.54
  833.5 0.6 multiply_reduce_fusion.2
  834.1 72.9 %psum.55 = f32[]{:T(128)} all-reduce(f32[]{:T(128)} %multiply_reduce_fusion.2), channel_id=1, replica_groups=mesh['path'=32,'mp'=2,'period'=4] {'path'}, use_global_device_ids=true, to_apply=%region_13.0 | all-reduce | flops 1 | bytes 8 | tf_op jit(solution)/shard_map/psum | solution.py:51
  907.7 0.6 divide_multiply_fusion
  908.5 1.4 multiply_add_fusion
  (28 shorter events, 2.5 us)
Async XLA Ops:
  7.2 87.7 %copy-start.1 = (s32[64]{0:T(128)S(1)}, s32[64]{0:T(128)}, u32[]{:S(2)}) copy-start(s32[64]{0:T(128)} %param.7) | copy-start | bytes 772
  7.2 234.3 %all-reduce.5.cloned.1.call-start = ((), (), s32[]{:S(2)}) async-start(), calls=%async_computation | async-start | bytes 2097152
  90.3 6.8 copy-start.3
  94.9 326.9 %copy-start.2 = (s32[64]{0:T(128)S(1)}, s32[64]{0:T(128)}, u32[]{:S(2)}) copy-start(s32[64]{0:T(128)} %param.6) | copy-start | bytes 772
  94.9 329.6 %copy-start = (f32[2048]{0:T(1024)S(1)}, f32[2048]{0:T(1024)}, u32[]{:S(2)}) copy-start(f32[2048]{0:T(1024)} %param.9) | copy-start | bytes 24580
  97.0 553.3 %all-reduce.7.cloned.1.call-start = ((), (), s32[]{:S(2)}) async-start(), calls=%async_computation.1 | async-start | bytes 2097152
Sparse Core Ops, SparseCore 0:
  97.1 144.2 all-reduce.4
  506.2 144.0 all-reduce.6
where the time goes:
time: 918 us; the launch traced here: 917 us
  blocking collectives  571 us (62%)
  waiting for transfers between devices  287 us (31%)
  matrix products  21.8 us (2%)
  between operations  19.3 us (2%)
  other arithmetic  10.3 us (1%)
    unnamed x4, waiting for transfers between devices  287 us
    psum x2, blocking collectives, col_norm(): return jnp.sqrt(lax.psum(jnp.sum(own * own), ('path', 'mp')) + 1e-12)  249 us
    psum x3, blocking collectives, row_norm(): return jnp.sqrt(lax.psum(jnp.sum(left * left), 'path') + 1e-12)  224 us
    all_gather x2, blocking collectives, on_device(): lax.all_gather(state.astype(jnp.bfloat16), 'path', axis=0, tiled=True)  92.6 us
  transfers between devices with their start and end apart: 2, of which 2 were waited for; matrix products, arithmetic and copies ran while one was open for 0% of the time, Pallas kernels for 0%

commit v1 on v0

--- a/solution.py
+++ b/solution.py
@@ -72,7 +72,11 @@
     rhobar = alpha
     solution = jnp.zeros_like(right)
     for step in range(ITERS):
-        half_b = lax.all_gather(state.astype(jnp.bfloat16), "path", axis=0, tiled=True)
+        part = state.astype(jnp.bfloat16)
+        size = lax.axis_size("path")
+        tiles_2 = jnp.stack([part for _ in range(size)])
+        tiles_2 = lax.all_to_all(tiles_2, "path", split_axis=0, concat_axis=0)
+        half_b = jnp.concatenate(tiles_2, axis=0)
         forward_picked = half_b.reshape(half_tiles, tile)[tile_cols]
         left = forward_prods(forward_picked) - alpha * left
         beta = row_norm(left)

time: 918 us -> 888 us (0.967)
  blocking collectives: 571 us -> 479 us
  waiting for transfers between devices: 287 us -> 321 us
  other arithmetic: 10.3 us -> 24.5 us
    all_gather x2 -> x0, blocking collectives: 92.6 us -> none  [on_device(): lax.all_gather(state.astype(jnp.bfloat16), 'path', axis=0, tiled=True)]
    all_to_all x0 -> x2, waiting for transfers between devices: none -> 33.6 us  [on_device(): tiles_2 = lax.all_to_all(tiles_2, 'path', split_axis=0, concat_axis=0)]
  transfers between devices with their start and end apart: 2 -> 4, of which waited for: 2 -> 4; matrix products, arithmetic and copies ran while one was open for 0% -> 0% of each run, Pallas kernels for 0% -> 0%
where the time goes in v1:
time: 888 us; the launch traced here: 887 us
  blocking collectives  479 us (54%)
  waiting for transfers between devices  321 us (36%)
  other arithmetic  24.5 us (3%)
  matrix products  21.9 us (2%)
  between operations  19.4 us (2%)
  local copies, waits for them, and re-layouts  12.8 us (1%)
    unnamed x4, waiting for transfers between devices  287 us
    psum x2, blocking collectives, col_norm(): return jnp.sqrt(lax.psum(jnp.sum(own * own), ('path', 'mp')) + 1e-12)  249 us
    psum x3, blocking collectives, row_norm(): return jnp.sqrt(lax.psum(jnp.sum(left * left), 'path') + 1e-12)  225 us
    all_to_all x2, waiting for transfers between devices, on_device(): tiles_2 = lax.all_to_all(tiles_2, 'path', split_axis=0, concat_axis=0)  33.6 us
  transfers between devices with their start and end apart: 4, of which 4 were waited for; matrix products, arithmetic and copies ran while one was open for 0% of the time, Pallas kernels for 0%

profile of v1, /device:TPU:8, one launch (start us, length us, event | category | flops | bytes accessed | tf_op | source)
XLA Modules:
  0.0 886.8 jit_solution(2605861206759245613)
XLA Ops:
  7.2 1.3 multiply_reduce_fusion.4
  8.5 78.3 %psum.49 = f32[]{:T(128)} all-reduce(f32[]{:T(128)} %multiply_reduce_fusion.4), channel_id=1, replica_groups=mesh['path'=32,'mp'=2,'period'=4] {'path'}, use_global_device_ids=true, to_apply=%region_1.0 | all-reduce | flops 1 | bytes 8 | tf_op jit(solution)/shard_map/psum | solution.py:51
  90.3 4.6 fusion.21
  95.4 1.6 copy.15
  98.3 143.1 %all-reduce.5.cloned.1.call-done = f32[262144]{0:T(1024)} async-done(((f32[262144]{0:T(1024)}), f32[262144]{0:T(1024)}) %all-reduce.5.cloned.1.call-update) | async-done | bytes 1048592
  241.4 1.4 multiply_reduce_fusion.1
  242.8 124.7 %psum.50 = f32[]{:T(128)} all-reduce(f32[]{:T(128)} %multiply_reduce_fusion.1), channel_id=1, replica_groups=mesh['path'=32,'mp'=2,'period'=4] {'path','mp'}, use_global_device_ids=true, to_apply=%region_4.0 | all-reduce | flops 1 | bytes 8 | tf_op jit(solution)/shard_map/psum | solution.py:54
  368.9 0.9 stack.4
  370.4 3.8 reduce.2
  374.2 1.2 reshape.98
  375.4 3.9 all-to-all-start
  379.6 16.8 %all-to-all-done = bf16[32,2,4096]{2,1,0:T(2,128)(2,1)S(1)} async-done(((bf16[32,2,4096]{2,1,0:T(2,128)(2,1)}), bf16[32,2,4096]{2,1,0:T(2,128)(2,1)S(1)}, u32[]{:S(2)}, u32[]{:S(2)}) %all-to-all-start) | async-done | bytes 524320 | tf_op jit(solution)/shard_map/all_to_all | solution.py:78
  396.9 3.2 reduce
  401.0 5.6 fusion.18
  406.8 2.5 psum.51
  409.9 73.1 %psum.52 = f32[]{:T(128)} all-reduce(f32[]{:T(128)} %get-tuple-element.2), channel_id=1, replica_groups=mesh['path'=32,'mp'=2,'period'=4] {'path'}, use_global_device_ids=true, to_apply=%region_7.0 | all-reduce | flops 1 | bytes 8 | tf_op jit(solution)/shard_map/psum | solution.py:51
  484.5 4.6 fusion.15
  489.6 1.5 copy.17
  491.2 144.2 %all-reduce.7.cloned.1.call-done = f32[262144]{0:T(1024)} async-done(((f32[262144]{0:T(1024)}), f32[262144]{0:T(1024)}) %all-reduce.7.cloned.1.call-update) | async-done | bytes 1048592
  635.4 1.4 multiply_reduce_fusion
  636.8 124.7 %psum.53 = f32[]{:T(128)} all-reduce(f32[]{:T(128)} %multiply_reduce_fusion), channel_id=1, replica_groups=mesh['path'=32,'mp'=2,'period'=4] {'path','mp'}, use_global_device_ids=true, to_apply=%region_10.0 | all-reduce | flops 1 | bytes 8 | tf_op jit(solution)/shard_map/psum | solution.py:54
  762.2 0.8 fusion.23
  763.0 0.9 stack.5
  763.9 3.9 reduce.3
  767.9 1.2 reshape.100
  769.1 4.1 all-to-all-start.1
  773.4 16.9 %all-to-all-done.1 = bf16[32,2,4096]{2,1,0:T(2,128)(2,1)S(1)} async-done(((bf16[32,2,4096]{2,1,0:T(2,128)(2,1)}), bf16[32,2,4096]{2,1,0:T(2,128)(2,1)S(1)}, u32[]{:S(2)}, u32[]{:S(2)}) %all-to-all-start.1) | async-done | bytes 524320 | tf_op jit(solution)/shard_map/all_to_all | solution.py:78
  790.7 3.3 reduce.1
  795.0 5.6 fusion.12
  800.8 2.5 psum.54
  804.0 73.2 %psum.55 = f32[]{:T(128)} all-reduce(f32[]{:T(128)} %multiply_reduce_fusion.2), channel_id=1, replica_groups=mesh['path'=32,'mp'=2,'period'=4] {'path'}, use_global_device_ids=true, to_apply=%region_13.0 | all-reduce | flops 1 | bytes 8 | tf_op jit(solution)/shard_map/psum | solution.py:51
  878.6 1.4 multiply_add_fusion
  (41 shorter events, 11.2 us)
Async XLA Ops:
  7.2 87.7 %copy-start.1 = (s32[64]{0:T(128)S(1)}, s32[64]{0:T(128)}, u32[]{:S(2)}) copy-start(s32[64]{0:T(128)} %param.7) | copy-start | bytes 772
  7.2 234.2 %all-reduce.5.cloned.1.call-start = ((), (), s32[]{:S(2)}) async-start(), calls=%async_computation.2 | async-start | bytes 2097152
  90.3 6.8 copy-start.3
  369.9 36.8 %copy-start.2 = (s32[64]{0:T(128)S(1)}, s32[64]{0:T(128)}, u32[]{:S(2)}) copy-start(s32[64]{0:T(128)} %param.6) | copy-start | bytes 772
  370.4 38.9 %copy-start = (f32[2048]{0:T(1024)S(1)}, f32[2048]{0:T(1024)}, u32[]{:S(2)}) copy-start(f32[2048]{0:T(1024)} %param.9) | copy-start | bytes 24580
  375.4 20.9 %all-to-all-start = ((bf16[32,2,4096]{2,1,0:T(2,128)(2,1)}), bf16[32,2,4096]{2,1,0:T(2,128)(2,1)S(1)}, u32[]{:S(2)}, u32[]{:S(2)}) async-start(bf16[32,2,4096]{2,1,0:T(2,128)(2,1)} %reshape.98), calls=%async_computation | async-start | bytes 1048576 | tf_op jit(solution)/shard_map/all_to_all | solution.py:78
  379.3 256.1 %all-reduce.7.cloned.1.call-start = ((), (), s32[]{:S(2)}) async-start(), calls=%async_computation.3 | async-start | bytes 2097152
  769.1 21.2 %all-to-all-start.1 = ((bf16[32,2,4096]{2,1,0:T(2,128)(2,1)}), bf16[32,2,4096]{2,1,0:T(2,128)(2,1)S(1)}, u32[]{:S(2)}, u32[]{:S(2)}) async-start(bf16[32,2,4096]{2,1,0:T(2,128)(2,1)} %reshape.100), calls=%async_computation.1 | async-start | bytes 1048576 | tf_op jit(solution)/shard_map/all_to_all | solution.py:78
Sparse Core Ops, SparseCore 0:
  97.1 144.2 all-reduce.4
  491.3 144.0 all-reduce.6
